TPU v7x, 256 devices: a whole 4x4x8 slice. The times are simulated.
256 devices in a mesh: dp: 16 (over z, x_lo), seq: 16 (over y, x_hi, core).
Axes of the slice: x: 4 (x_hi: 2, x_lo: 2; x = x_hi * 2 + x_lo), y: 4, z: 8, core: 2. Of those that a mesh axis runs over, the one named last changes fastest.
Arguments:
- states: bfloat16 [16, 1024, 4096], P('dp', 'seq'), may hold values from -6 to 6
- kv_weight: bfloat16 [4096, 1536], P('seq'), may hold values from -0.09375 to 0.09375
- queries: bfloat16 [16, 4096, 768], P('dp', 'seq'), may hold values from -150 to 150
- hidden: bfloat16 [16, 4096, 1536], P('dp', 'seq'), may hold values from -3 to 3
- out_proj: bfloat16 [768, 1536], P('seq'), may hold values from -0.21875 to 0.21875
- disc_in: bfloat16 [1536, 1024], replicated, may hold values from -0.15625 to 0.15625
- conv_weight: bfloat16 [41, 64, 1024], replicated, may hold values from -0.125 to 0.125
- score_weight: float32 [1024], replicated, may hold values from -0.1875 to 0.1875
- frame_len: int32 [16], replicated, may hold values from 1024 to 4096, as said below
- state_len: int32 [16], replicated, may hold values from 256 to 1024, as said below
Outputs:
- grad_out_proj: float32 [768, 1536], P('seq')
- loss_mean: float32 [], replicated
Inputs may be any that keep to these rules, and one draw needn't show every extreme that they name: `frame_len`: one clip has all 4096 frames live in every draw. `state_len`: one clip has all 1024 backbone frames live in every draw.
All inputs are finite; a program needn't handle non-finite values.
Results may differ from a plain program's by a relative error of at most 0.005.
Values may be sent and summed in bfloat16 or wider, within the bound.
No kernel may reach another device: no remote copies, remote signals or barrier semaphores. Data moves between devices by JAX's collectives and lax.ppermute only.
A program may use at most 128 MiB of HBM per device.

v0:
```python
import math
import jax
import jax.numpy as jnp
from jax import lax
from jax.sharding import PartitionSpec as P

HEAD_DIM = 128
GROUPS = 16
STRIDE = 4


def with_halo(array, sides, width):
    for axis, dim in sides:
        size, length = (lax.axis_size(axis), array.shape[dim])
        up = [(i, (i + 1) % size) for i in range(size - 1)]
        down = [(j, i) for i, j in up]
        last = lax.slice_in_dim(array, length - width, length, axis=dim)
        initial = lax.slice_in_dim(array, 0, width, axis=dim)
        before = lax.ppermute(last, axis, up)
        after = lax.ppermute(initial, axis, down)
        array = jnp.concatenate([before, array, after], axis=dim)
    return array


def regroup(weight_taps, group_count):
    kernel, group_in, channels = weight_taps.shape
    blocks = weight_taps.reshape(kernel, group_in, group_count, channels // group_count)
    turned = jnp.transpose(blocks, (0, 3, 2, 1)).reshape(kernel, channels // group_count, channels)
    return jnp.flip(turned, 0)


def disc_conv(padded, weight_taps, group_count, stride):
    return lax.conv_general_dilated(
        padded[None],
        weight_taps,
        (stride,),
        "VALID",
        dimension_numbers=("NWC", "WIO", "NWC"),
        feature_group_count=group_count,
        preferred_element_type=jnp.float32,
    )[0]


def disc_back(grad_wide, flipped, group_count, stride, high_pad):
    return lax.conv_general_dilated(
        grad_wide[None],
        flipped,
        (1,),
        [(0, high_pad)],
        lhs_dilation=(stride,),
        dimension_numbers=("NWC", "WIO", "NWC"),
        feature_group_count=group_count,
        preferred_element_type=jnp.float32,
    )[0]


def attend(query, keys_values, live_keys):
    row_count, att_width = query.shape
    head_count = att_width // HEAD_DIM
    query_heads = query.astype(jnp.float32).reshape(row_count, head_count, HEAD_DIM)
    key_heads = keys_values[:, :att_width].reshape(-1, head_count, HEAD_DIM)
    value_heads = keys_values[:, att_width:].reshape(-1, head_count, HEAD_DIM)
    scores = jnp.einsum(
        "qhd,khd->hqk", query_heads, key_heads, precision=lax.Precision.HIGHEST
    ) / math.sqrt(HEAD_DIM)
    scores = jnp.where(live_keys[None, None, :], scores, -1e30)
    row_max = jnp.max(scores, axis=2, keepdims=True)
    expo_scores = jnp.where(live_keys[None, None, :], jnp.exp(scores - row_max), 0.0)
    denom = jnp.sum(expo_scores, axis=2)
    weights = expo_scores.astype(jnp.bfloat16)
    mixed_heads = jnp.einsum(
        "hqk,khd->qhd", weights.astype(jnp.float32), value_heads, precision=lax.Precision.HIGHEST
    )
    mixed_heads = mixed_heads / jnp.transpose(denom)[:, :, None]
    return mixed_heads.reshape(row_count, att_width).astype(jnp.bfloat16)


def shards(
    states,
    kv_weight,
    queries,
    hidden,
    out_proj,
    disc_in,
    conv_weight,
    score_weight,
    frame_len,
    state_len,
):
    states_local = states[0]
    frame_count = hidden.shape[1]
    clip_index = lax.axis_index("dp")
    seq_index = lax.axis_index("seq")
    clip_pick = jnp.arange(frame_len.shape[0]) == clip_index
    clip_frames = jnp.sum(jnp.where(clip_pick, frame_len, 0))
    clip_states = jnp.sum(jnp.where(clip_pick, state_len, 0))
    sliced = states_local
    projected = jnp.dot(
        sliced,
        lax.all_gather(kv_weight, "seq", axis=0, tiled=True),
        preferred_element_type=jnp.float32,
    )
    keys_values = lax.all_gather(projected, "seq", axis=0, tiled=True)
    live_keys = jnp.arange(keys_values.shape[0]) < clip_states
    attended = attend(queries[0], keys_values, live_keys)
    sliced = attended
    lifted = hidden[0].astype(jnp.float32) + jnp.dot(
        sliced,
        lax.all_gather(out_proj, "seq", axis=0, tiled=True),
        preferred_element_type=jnp.float32,
    )
    mixed_rows = lifted.astype(jnp.bfloat16)
    frame_ids = seq_index * frame_count + jnp.arange(frame_count)
    inside = (frame_ids < clip_frames)[:, None]
    disc_feed = jnp.where(
        inside, jnp.dot(mixed_rows, disc_in, preferred_element_type=jnp.float32), 0.0
    ).astype(jnp.bfloat16)
    margin_rows = (conv_weight.shape[0] - 1) // 2
    padded = with_halo(disc_feed, (("seq", 0),), margin_rows)
    pre = disc_conv(padded, conv_weight, GROUPS, STRIDE)
    sigmoid_pre = jax.nn.sigmoid(pre)
    critic = jnp.dot(pre * sigmoid_pre, score_weight, precision=lax.Precision.HIGHEST)
    out_count = pre.shape[0]
    valid_out = STRIDE * (seq_index * out_count + jnp.arange(out_count)) < clip_frames
    shortfall = 1.0 - critic
    local_loss = jnp.sum(jnp.where(valid_out, shortfall * shortfall, 0.0))
    push_score = jnp.where(valid_out, -2.0 * shortfall, 0.0)
    slope_pre = sigmoid_pre * (1.0 + pre * (1.0 - sigmoid_pre))
    grad_pre = (push_score[:, None] * score_weight[None, :] * slope_pre).astype(jnp.bfloat16)
    reach_out = margin_rows // STRIDE
    grad_wide = with_halo(grad_pre, (("seq", 0),), reach_out)
    grad_feed = disc_back(grad_wide, regroup(conv_weight, GROUPS), GROUPS, STRIDE, STRIDE - 1)
    grad_feed = jnp.where(inside, grad_feed, 0.0).astype(jnp.bfloat16)
    grad_mixed = lax.dot_general(
        grad_feed, disc_in, (((1,), (1,)), ((), ())), preferred_element_type=jnp.float32
    ).astype(jnp.bfloat16)
    full_term = lax.dot_general(
        attended, grad_mixed, (((0,), (0,)), ((), ())), preferred_element_type=jnp.float32
    )
    summed_clips = lax.psum(full_term, "dp")
    grad_proj = lax.psum_scatter(summed_clips, "seq", scatter_dimension=0, tiled=True)
    total_loss = lax.psum(local_loss, ("dp", "seq"))
    counted = jnp.sum((frame_len + STRIDE - 1) // STRIDE).astype(jnp.float32)
    return (grad_proj, total_loss / counted)


def solution(mesh):
    return jax.shard_map(
        shards,
        mesh=mesh,
        in_specs=(
            P("dp", "seq", None),
            P("seq", None),
            P("dp", "seq", None),
            P("dp", "seq", None),
            P("seq", None),
            P(),
            P(),
            P(),
            P(),
            P(),
        ),
        out_specs=(P("seq", None), P()),
        check_vma=False,
    )
```

profile of v0, /device:TPU:8, one launch (start us, length us, event | category | flops | bytes accessed | tf_op | source)
XLA Modules:
  0.0 666.0 jit_solution(14477105413284666974)
XLA Ops:
  7.2 0.0 copy-start
  7.2 0.0 all-gather.4.cloned.1.call-start
  7.2 0.7 all-gather.4.cloned.1.call-update
  7.9 0.0 copy-start.7
  7.9 0.0 copy-start.8
  7.9 0.0 all-gather.6.cloned.1.call-start
  8.0 100.1 %all-gather.4.cloned.1.call-done = bf16[4096,1536]{1,0:T(8,128)(2,1)} async-done(((bf16[256,1536]{1,0:T(8,128)(2,1)}), bf16[4096,1536]{1,0:T(8,128)(2,1)}) %all-gather.4.cloned.1.call-update) | async-done | bytes 12582928 | tf_op jit(solution)/shard_map/all_gather | solution.py:100
  108.1 7.8 %fusion.31 = f32[64,1536]{1,0:T(8,128)} fusion(bf16[4096,1536]{1,0:T(8,128)(2,1)} %all-gather.4.cloned.1.call-done, bf16[1,64,4096]{2,1,0:T(8,128)(2,1)} %param.10), kind=kOutput, calls=%fused_computation.30 | convolution fusion | flops 805306368 | bytes 13500416 | tf_op jit(solution)/shard_map/dot_general | solution.py:98
  115.8 0.0 all-gather.6.cloned.1.call-update
  115.9 0.0 all-gather.8.cloned.1.call-start
  115.9 0.7 all-gather.8.cloned.1.call-update
  116.6 0.0 reduce-scatter.2.cloned.1.call-start
  116.7 1.2 copy.20
  117.8 0.0 copy-done.7
  117.8 0.0 copy-done.8
  117.8 0.7 fusion.42
  118.6 0.7 add_compare_fusion
  119.2 0.0 copy-start.5
  119.2 0.7 iota_compare_fusion
  119.9 63.1 %all-gather.6.cloned.1.call-done = f32[1024,1536]{1,0:T(8,128)} async-done(((f32[64,1536]{1,0:T(8,128)}), f32[1024,1536]{1,0:T(8,128)}) %all-gather.6.cloned.1.call-update) | async-done | bytes 6291472 | tf_op jit(solution)/shard_map/all_gather | solution.py:103
  183.0 5.9 fusion.48
  188.9 3.5 copy.19
  192.5 3.6 copy.18
  196.0 4.6 fusion.52
  200.6 0.0 copy-start.1
  200.6 2.4 fusion.51
  203.1 1.7 fusion.24
  204.8 33.3 %all-gather.8.cloned.1.call-done = bf16[768,1536]{1,0:T(8,128)(2,1)} async-done(((bf16[48,1536]{1,0:T(8,128)(2,1)}), bf16[768,1536]{1,0:T(8,128)(2,1)}) %all-gather.8.cloned.1.call-update) | async-done | bytes 2359312 | tf_op jit(solution)/shard_map/all_gather | solution.py:109
  238.1 4.3 fusion.23
  242.4 1.5 fusion.49
  243.8 2.2 collective-permute-start
  246.0 5.8 collective-permute-start.1
  251.8 14.8 %shard_map.115 = bf16[41,64,16,64]{3,2,1,0:T(8,128)(2,1)} reshape(bf16[41,64,1024]{2,1,0:T(8,128)(2,1)} %param.16) | data formatting | bytes 10747904 | tf_op jit(solution)/shard_map/shard_map
  266.6 0.0 collective-permute-done
  266.6 0.0 collective-permute-done.1
  266.6 2.0 pad_maximum_fusion
  268.6 2.3 copy.24
  270.9 6.3 copy.25
  277.2 0.0 copy-start.4
  277.2 18.9 %fusion.27 = f32[64,16,64]{2,1,0:T(8,128)} fusion(bf16[1,296,16,64]{3,0,2,1:T(2,128)(2,1)} %copy.25, bf16[41,64,16,64]{3,2,1,0:T(8,128)(2,1)} %shard_map.115), kind=kOutput, calls=%fused_computation.25 | convolution fusion | flops 343932928 | bytes 6242304 | tf_op jit(solution)/shard_map/conv_general_dilated | solution.py:33
  296.1 1.2 squeeze.12
  297.3 1.6 fusion.41
  298.9 0.1 multiply_convert_fusion
  299.1 1.9 collective-permute-start.2
  301.0 6.0 collective-permute-start.3
  307.1 19.1 %copy.27 = bf16[41,64,16,64]{1,2,3,0:T(8,128)(2,1)} copy(bf16[41,64,16,64]{3,2,1,0:T(8,128)(2,1)} %shard_map.115) | data formatting | bytes 10747904 | tf_op jit(solution)/shard_map/shard_map
  326.2 15.0 %reshape.48 = bf16[41,64,1024]{2,1,0:T(8,128)(2,1)} reshape(bf16[41,64,16,64]{3,2,1,0:T(8,128)(2,1)} %bitcast.55) | data formatting | bytes 10747904 | tf_op jit(solution)/shard_map/reshape | solution.py:28
  341.2 5.9 rev.6
  347.1 14.8 %rev.7 = bf16[41,64,16,64]{3,2,1,0:T(8,128)(2,1)} reshape(bf16[41,64,1024]{2,1,0:T(8,128)(2,1)} %rev.6) | data formatting | bytes 10747904 | tf_op jit(solution)/shard_map/jit(_flip)/rev | solution.py:29
  361.9 0.0 collective-permute-done.2
  361.9 0.0 collective-permute-done.3
  362.0 1.2 broadcast_in_dim.69
  363.2 54.6 %fusion.1 = bf16[1,256,16,64]{3,0,2,1:T(2,128)(2,1)} fusion(bf16[1,74,16,64]{3,0,2,1:T(2,128)(2,1)} %broadcast_in_dim.69, bf16[41,64,16,64]{3,2,1,0:T(8,128)(2,1)} %rev.7), kind=kOutput, calls=%fused_computation.1 | convolution fusion | flops 343932928 | bytes 6049792 | tf_op jit(solution)/shard_map/conv_general_dilated | solution.py:45
  417.8 5.7 copy.30
  423.5 2.1 copy.31
  425.5 0.0 copy-done.6
  425.5 4.8 fusion.16
  430.3 0.0 reduce-scatter.2.cloned.1.call-update
  430.4 0.0 all-reduce.2.cloned.1.call-start
  430.4 88.9 %reduce-scatter.2.cloned.1.call-done = f32[48,1536]{1,0:T(8,128)} async-done(((f32[768,1536]{1,0:T(8,128)}), f32[48,1536]{1,0:T(8,128)}) %reduce-scatter.2.cloned.1.call-update) | async-done | bytes 294928 | tf_op jit(solution)/shard_map/reduce_scatter | solution.py:141
  519.3 0.0 all-reduce.2.cloned.1.call-update
  520.0 74.0 %psum.15 = f32[]{:T(128)} all-reduce(f32[]{:T(128)} %get-tuple-element.10), channel_id=1, replica_groups=mesh['dp'=16,'seq'=16] {'dp','seq'}, use_global_device_ids=true, to_apply=%region_7.8 | all-reduce | flops 1 | bytes 8 | tf_op jit(solution)/shard_map/psum | solution.py:142
  594.7 61.6 %all-reduce.2.cloned.1.call-done = f32[48,1536]{1,0:T(8,128)} async-done(((f32[48,1536]{1,0:T(8,128)}), f32[48,1536]{1,0:T(8,128)}) %all-reduce.2.cloned.1.call-update) | async-done | bytes 294928 | tf_op jit(solution)/shard_map/psum | solution.py:140
  656.3 1.7 copy.42
  (11 shorter events, 0.1 us)
Async XLA Ops:
  7.2 231.0 %copy-start = (bf16[1536,1024]{1,0:T(8,128)(2,1)S(1)}, bf16[1536,1024]{1,0:T(8,128)(2,1)}, u32[]{:S(2)}) copy-start(bf16[1536,1024]{1,0:T(8,128)(2,1)} %param.15) | copy-start | bytes 9437188
  7.2 100.9 %all-gather.4.cloned.1.call-start = ((), (), s32[]{:S(2)}) async-start(), calls=%async_computation.1 | async-start | bytes 13369344 | tf_op jit(solution)/shard_map/all_gather | solution.py:100
  7.9 109.9 %copy-start.7 = (s32[16]{0:T(128)S(1)}, s32[16]{0:T(128)}, u32[]{:S(2)}) copy-start(s32[16]{0:T(128)} %param.18) | copy-start | bytes 196
  7.9 109.9 %copy-start.8 = (s32[16]{0:T(128)S(1)}, s32[16]{0:T(128)}, u32[]{:S(2)}) copy-start(s32[16]{0:T(128)} %param.19) | copy-start | bytes 196
  7.9 175.1 %all-gather.6.cloned.1.call-start = ((), (), s32[]{:S(2)}) async-start(), calls=%async_computation.2 | async-start | bytes 6684672 | tf_op jit(solution)/shard_map/all_gather | solution.py:103
  115.9 122.3 %all-gather.8.cloned.1.call-start = ((), (), s32[]{:S(2)}) async-start(), calls=%async_computation.3 | async-start | bytes 2506752 | tf_op jit(solution)/shard_map/all_gather | solution.py:109
  116.6 402.7 %reduce-scatter.2.cloned.1.call-start = ((), (), s32[]{:S(2)}) async-start(), calls=%async_computation.4 | async-start | bytes 5013504 | tf_op jit(solution)/shard_map/reduce_scatter | solution.py:141
  119.2 118.9 %copy-start.5 = (pred[256]{0:T(512)(128)(4,1)}, pred[256]{0:T(512)(128)(4,1)S(1)}, u32[]{:S(2)}) copy-start(pred[256]{0:T(512)(128)(4,1)S(1)} %add_compare_fusion) | copy-start | bytes 772
  200.6 2.4 copy-start.1
  204.8 37.6 %copy-start.2 = (bf16[256,6,128]{0,2,1:T(8,128)(2,1)}, bf16[256,6,128]{0,2,1:T(8,128)(2,1)S(1)}, u32[]{:S(2)}) copy-start(bf16[256,6,128]{0,2,1:T(8,128)(2,1)S(1)} %fusion.24) | copy-start | bytes 1179652
  243.8 22.7 %collective-permute-start = (bf16[20,1024]{1,0:T(8,128)(2,1)}, bf16[20,1024]{1,0:T(8,128)(2,1)S(1)}, u32[]{:S(2)}, u32[]{:S(2)}) collective-permute-start(bf16[20,1024]{1,0:T(8,128)(2,1)} %get-tuple-element.6), channel_id=1, source_target_pairs={{0,1},{1,2},{2,3},{3,4},{4,5},{5,6},{6,7},{7,8},{8,9},{9,10},{10,1... | collective-permute-start | bytes 122888 | tf_op jit(solution)/shard_map/ppermute | solution.py:19
  246.0 20.6 %collective-permute-start.1 = (bf16[20,1024]{1,0:T(8,128)(2,1)}, bf16[20,1024]{1,0:T(8,128)(2,1)S(1)}, u32[]{:S(2)}, u32[]{:S(2)}) collective-permute-start(bf16[20,1024]{1,0:T(8,128)(2,1)} %get-tuple-element.7), channel_id=1, source_target_pairs={{1,0},{2,1},{3,2},{4,3},{5,4},{6,5},{7,6},{8,7},{9,8},{10,9},{11,1... | collective-permute-start | bytes 122888 | tf_op jit(solution)/shard_map/ppermute | solution.py:20
  277.2 20.1 %copy-start.4 = (f32[1024]{0:T(1024)S(1)}, f32[1024]{0:T(1024)}, u32[]{:S(2)}) copy-start(f32[1024]{0:T(1024)} %param.17) | copy-start | bytes 12292
  299.1 62.8 %collective-permute-start.2 = (bf16[5,1024]{1,0:T(8,128)(2,1)S(1)}, bf16[5,1024]{1,0:T(8,128)(2,1)S(1)}, u32[]{:S(2)}, u32[]{:S(2)}) collective-permute-start(bf16[5,1024]{1,0:T(8,128)(2,1)S(1)} %get-tuple-element.8), channel_id=1, source_target_pairs={{0,1},{1,2},{2,3},{3,4},{4,5},{5,6},{6,7},{7,8},{8,9},{9,10},{10,1... | collective-permute-start | bytes 30728 | tf_op jit(solution)/shard_map/ppermute | solution.py:19
  301.0 60.9 %collective-permute-start.3 = (bf16[5,1024]{1,0:T(8,128)(2,1)S(1)}, bf16[5,1024]{1,0:T(8,128)(2,1)S(1)}, u32[]{:S(2)}, u32[]{:S(2)}) collective-permute-start(bf16[5,1024]{1,0:T(8,128)(2,1)S(1)} %get-tuple-element.9), channel_id=1, source_target_pairs={{1,0},{2,1},{3,2},{4,3},{5,4},{6,5},{7,6},{8,7},{9,8},{10,9},{11,1... | collective-permute-start | bytes 30728 | tf_op jit(solution)/shard_map/ppermute | solution.py:20
  417.8 7.7 %copy-start.3 = (bf16[256,6,128]{0,2,1:T(8,128)(2,1)S(1)}, bf16[256,6,128]{0,2,1:T(8,128)(2,1)}, u32[]{:S(2)}) copy-start(bf16[256,6,128]{0,2,1:T(8,128)(2,1)} %copy-done.2) | copy-start | bytes 1179652
  417.8 7.7 %copy-start.6 = (pred[256]{0:T(512)(128)(4,1)S(1)}, pred[256]{0:T(512)(128)(4,1)}, u32[]{:S(2)}) copy-start(pred[256]{0:T(512)(128)(4,1)} %copy-done.5) | copy-start | bytes 772
  430.4 225.9 %all-reduce.2.cloned.1.call-start = ((), (), s32[]{:S(2)}) async-start(), calls=%async_computation.5 | async-start | bytes 589824 | tf_op jit(solution)/shard_map/psum | solution.py:140
Sparse Core Ops, SparseCore 0:
  10.8 97.2 all-gather.3
  116.0 66.9 all-gather.5
  185.8 52.2 all-gather.7
  430.5 88.7 reduce-scatter.1
  522.0 134.2 all-reduce.1
where the time goes:
time: 678 us; the launch traced here: 666 us
  waiting for transfers between devices  348 us (51%)
  local copies, waits for them, and re-layouts  106 us (16%)
  matrix products  98.3 us (14%)
  blocking collectives  74 us (11%)
  between operations  16.8 us (2%)
  starting transfers between devices  16.1 us (2%)
    all_gather x1, waiting for transfers between devices, shards(): lax.all_gather(kv_weight, 'seq', axis=0, tiled=True)  100 us
    reduce_scatter x1, waiting for transfers between devices, shards(): lax.psum_scatter(summed_clips, 'seq', scatter_dimension=0, tiled=True)  88.9 us
    psum x1, blocking collectives, shards(): total_loss = lax.psum(local_loss, ('dp', 'seq'))  74 us
    all_gather x1, waiting for transfers between devices, shards(): keys_values = lax.all_gather(projected, 'seq', axis=0, tiled=True)  63.1 us
    psum x1, waiting for transfers between devices, shards(): summed_clips = lax.psum(full_term, 'dp')  61.6 us
    conv_general_dilated x1, matrix products, disc_back(): lax.conv_general_dilated(grad_wide[None], flipped, (1,), [(0, high_pad)],...  54.6 us
    another operation x2, local copies, waits for them, and re-layouts  33.9 us
    all_gather x1, waiting for transfers between devices, shards(): lax.all_gather(out_proj, 'seq', axis=0, tiled=True)  33.3 us
  transfers between devices with their start and end apart: 9, of which 5 were waited for; matrix products, arithmetic and copies ran while one was open for 14% of the time, Pallas kernels for 0%

commit v1 on v0

--- a/solution.py
+++ b/solution.py
@@ -7,6 +7,11 @@
 HEAD_DIM = 128
 GROUPS = 16
 STRIDE = 4
+
+
+def swapped_in(value, name, d):
+    repeated = jnp.stack([value] * lax.axis_size(name))
+    return jnp.concatenate(lax.all_to_all(repeated, name, 0, 0), axis=d)
 
 
 def with_halo(array, sides, width):
@@ -95,11 +100,7 @@
     clip_frames = jnp.sum(jnp.where(clip_pick, frame_len, 0))
     clip_states = jnp.sum(jnp.where(clip_pick, state_len, 0))
     sliced = states_local
-    projected = jnp.dot(
-        sliced,
-        lax.all_gather(kv_weight, "seq", axis=0, tiled=True),
-        preferred_element_type=jnp.float32,
-    )
+    projected = jnp.dot(sliced, swapped_in(kv_weight, "seq", 0), preferred_element_type=jnp.float32)
     keys_values = lax.all_gather(projected, "seq", axis=0, tiled=True)
     live_keys = jnp.arange(keys_values.shape[0]) < clip_states
     attended = attend(queries[0], keys_values, live_keys)

time: 678 us -> 720 us (1.062)
  blocking collectives: 74 us -> 221 us
  waiting for transfers between devices: 348 us -> 252 us
    all_to_all x0 -> x1, blocking collectives: none -> 147 us  [swapped_in(): return jnp.concatenate(lax.all_to_all(repeated, name, 0, 0), axis=d)]
    all_gather x1 -> x0, waiting for transfers between devices: 100 us -> none  [shards(): lax.all_gather(kv_weight, 'seq', axis=0, tiled=True)]
    another operation x2 -> x3, local copies, waits for them, and re-layouts: 33.9 us -> 40.9 us
  transfers between devices with their start and end apart: 9 -> 8, of which waited for: 5 -> 4; matrix products, arithmetic and copies ran while one was open for 14% -> 13% of each run, Pallas kernels for 0% -> 0%
where the time goes in v1:
time: 720 us; the launch traced here: 715 us
  waiting for transfers between devices  252 us (35%)
  blocking collectives  221 us (31%)
  local copies, waits for them, and re-layouts  113 us (16%)
  matrix products  93.5 us (13%)
  between operations  16.6 us (2%)
  starting transfers between devices  13.1 us (2%)
    all_to_all x1, blocking collectives, swapped_in(): return jnp.concatenate(lax.all_to_all(repeated, name, 0, 0), axis=d)  147 us
    reduce_scatter x1, waiting for transfers between devices, shards(): lax.psum_scatter(summed_clips, 'seq', scatter_dimension=0, tiled=True)  92 us
    psum x1, blocking collectives, shards(): total_loss = lax.psum(local_loss, ('dp', 'seq'))  74 us
    all_gather x1, waiting for transfers between devices, shards(): keys_values = lax.all_gather(projected, 'seq', axis=0, tiled=True)  64.4 us
    psum x1, waiting for transfers between devices, shards(): summed_clips = lax.psum(full_term, 'dp')  61.6 us
    conv_general_dilated x1, matrix products, disc_back(): lax.conv_general_dilated(grad_wide[None], flipped, (1,), [(0, high_pad)],...  54.6 us
    another operation x2, local copies, waits for them, and re-layouts  33.9 us
    all_gather x1, waiting for transfers between devices, shards(): lax.all_gather(out_proj, 'seq', axis=0, tiled=True)  33.3 us
  transfers between devices with their start and end apart: 8, of which 4 were waited for; matrix products, arithmetic and copies ran while one was open for 13% of the time, Pallas kernels for 0%

profile of v1, /device:TPU:8, one launch (start us, length us, event | category | flops | bytes accessed | tf_op | source)
XLA Modules:
  0.0 715.1 jit_solution(16003585780314225475)
XLA Ops:
  7.2 0.0 copy-start
  7.2 0.0 all-gather.3.cloned.1.call-start
  7.2 7.1 stack.2
  14.3 146.5 %all_to_all.5 = bf16[16,256,1536]{2,1,0:T(8,128)(2,1)S(1)} all-to-all(bf16[16,256,1536]{2,1,0:T(8,128)(2,1)} %stack.2), channel_id=1, replica_groups=mesh['dp'=16,'seq'=16] {'seq'}, dimensions={0} | all-to-all | bytes 25165824 | tf_op jit(solution)/shard_map/all_to_all | solution.py:14
  160.8 0.0 copy-done.4
  160.8 3.0 fusion.31
  163.8 0.0 all-gather.3.cloned.1.call-update
  163.8 0.0 all-gather.5.cloned.1.call-start
  163.9 0.7 all-gather.5.cloned.1.call-update
  164.6 0.5 reduce-scatter.2.cloned.1.call-start
  165.1 1.2 copy.20
  166.3 0.0 copy-done.8
  166.3 0.0 copy-done.9
  166.3 0.7 fusion.42
  167.0 0.7 add_compare_fusion
  167.7 0.0 copy-start.6
  167.7 0.7 iota_compare_fusion
  168.4 64.4 %all-gather.3.cloned.1.call-done = f32[1024,1536]{1,0:T(8,128)} async-done(((f32[64,1536]{1,0:T(8,128)}), f32[1024,1536]{1,0:T(8,128)}) %all-gather.3.cloned.1.call-update) | async-done | bytes 6291472 | tf_op jit(solution)/shard_map/all_gather | solution.py:104
  232.7 5.9 fusion.48
  238.6 3.5 copy.18
  242.2 3.6 copy.19
  245.7 4.6 fusion.52
  250.4 0.0 copy-start.1
  250.4 2.4 fusion.51
  252.8 0.0 copy-done.1
  252.8 1.7 fusion.24
  254.5 0.0 copy-start.2
  254.5 33.3 %all-gather.5.cloned.1.call-done = bf16[768,1536]{1,0:T(8,128)(2,1)} async-done(((bf16[48,1536]{1,0:T(8,128)(2,1)}), bf16[768,1536]{1,0:T(8,128)(2,1)}) %all-gather.5.cloned.1.call-update) | async-done | bytes 2359312 | tf_op jit(solution)/shard_map/all_gather | solution.py:110
  287.8 4.3 fusion.23
  292.1 0.0 copy-done.2
  292.1 1.5 fusion.49
  293.6 2.6 collective-permute-start.1
  296.1 1.9 collective-permute-start
  298.1 14.8 %shard_map.115 = bf16[41,64,16,64]{3,2,1,0:T(8,128)(2,1)} reshape(bf16[41,64,1024]{2,1,0:T(8,128)(2,1)} %param.16) | data formatting | bytes 10747904 | tf_op jit(solution)/shard_map/shard_map
  312.8 0.0 collective-permute-done.1
  312.8 0.0 collective-permute-done
  312.8 2.0 pad_maximum_fusion
  314.9 2.3 copy.24
  317.1 6.3 copy.25
  323.5 0.0 copy-start.5
  323.5 18.9 %fusion.27 = f32[64,16,64]{2,1,0:T(8,128)} fusion(bf16[1,296,16,64]{3,0,2,1:T(2,128)(2,1)} %copy.25, bf16[41,64,16,64]{3,2,1,0:T(8,128)(2,1)} %shard_map.115), kind=kOutput, calls=%fused_computation.25 | convolution fusion | flops 343932928 | bytes 6242304 | tf_op jit(solution)/shard_map/conv_general_dilated | solution.py:38
  342.4 1.2 squeeze.12
  343.5 1.7 fusion.41
  345.2 0.1 multiply_convert_fusion
  345.3 6.0 collective-permute-start.3
  351.4 1.9 collective-permute-start.2
  353.3 19.1 %copy.27 = bf16[41,64,16,64]{1,2,3,0:T(8,128)(2,1)} copy(bf16[41,64,16,64]{3,2,1,0:T(8,128)(2,1)} %shard_map.115) | data formatting | bytes 10747904 | tf_op jit(solution)/shard_map/shard_map
  372.4 15.0 %reshape.54 = bf16[41,64,1024]{2,1,0:T(8,128)(2,1)} reshape(bf16[41,64,16,64]{3,2,1,0:T(8,128)(2,1)} %bitcast.57) | data formatting | bytes 10747904 | tf_op jit(solution)/shard_map/reshape | solution.py:33
  387.5 5.9 rev.6
  393.4 14.8 %rev.7 = bf16[41,64,16,64]{3,2,1,0:T(8,128)(2,1)} reshape(bf16[41,64,1024]{2,1,0:T(8,128)(2,1)} %rev.6) | data formatting | bytes 10747904 | tf_op jit(solution)/shard_map/jit(_flip)/rev | solution.py:34
  408.2 0.0 collective-permute-done.3
  408.2 0.0 collective-permute-done.2
  408.2 1.2 broadcast_in_dim.69
  409.4 54.6 %fusion.1 = bf16[1,256,16,64]{3,0,2,1:T(2,128)(2,1)} fusion(bf16[1,74,16,64]{3,0,2,1:T(2,128)(2,1)} %broadcast_in_dim.69, bf16[41,64,16,64]{3,2,1,0:T(8,128)(2,1)} %rev.7), kind=kOutput, calls=%fused_computation.1 | convolution fusion | flops 343932928 | bytes 6049792 | tf_op jit(solution)/shard_map/conv_general_dilated | solution.py:50
  464.0 5.7 copy.30
  469.7 2.1 copy.31
  471.8 4.8 fusion.16
  476.5 0.0 reduce-scatter.2.cloned.1.call-update
  476.6 0.0 all-reduce.2.cloned.1.call-start
  476.6 92.0 %reduce-scatter.2.cloned.1.call-done = f32[48,1536]{1,0:T(8,128)} async-done(((f32[768,1536]{1,0:T(8,128)}), f32[48,1536]{1,0:T(8,128)}) %reduce-scatter.2.cloned.1.call-update) | async-done | bytes 294928 | tf_op jit(solution)/shard_map/reduce_scatter | solution.py:142
  568.6 0.0 all-reduce.2.cloned.1.call-update
  569.2 74.0 %psum.15 = f32[]{:T(128)} all-reduce(f32[]{:T(128)} %get-tuple-element.10), channel_id=1, replica_groups=mesh['dp'=16,'seq'=16] {'dp','seq'}, use_global_device_ids=true, to_apply=%region_7.8 | all-reduce | flops 1 | bytes 8 | tf_op jit(solution)/shard_map/psum | solution.py:143
  643.9 61.6 %all-reduce.2.cloned.1.call-done = f32[48,1536]{1,0:T(8,128)} async-done(((f32[48,1536]{1,0:T(8,128)}), f32[48,1536]{1,0:T(8,128)}) %all-reduce.2.cloned.1.call-update) | async-done | bytes 294928 | tf_op jit(solution)/shard_map/psum | solution.py:141
  705.5 1.7 copy.42
  (12 shorter events, 0.1 us)
Async XLA Ops:
  7.2 280.7 %copy-start = (bf16[1536,1024]{1,0:T(8,128)(2,1)S(1)}, bf16[1536,1024]{1,0:T(8,128)(2,1)}, u32[]{:S(2)}) copy-start(bf16[1536,1024]{1,0:T(8,128)(2,1)} %param.15) | copy-start | bytes 9437188
  7.2 225.6 %all-gather.3.cloned.1.call-start = ((), (), s32[]{:S(2)}) async-start(), calls=%async_computation.2 | async-start | bytes 6684672 | tf_op jit(solution)/shard_map/all_gather | solution.py:104
  14.3 146.5 %copy-start.4 = (bf16[1,64,4096]{2,1,0:T(8,128)(2,1)S(1)}, bf16[1,64,4096]{2,1,0:T(8,128)(2,1)}, u32[]{:S(2)}) copy-start(bf16[1,64,4096]{2,1,0:T(8,128)(2,1)} %param.10) | copy-start | bytes 1572868
  160.8 5.5 copy-start.8
  160.8 5.5 copy-start.9
  163.8 124.0 %all-gather.5.cloned.1.call-start = ((), (), s32[]{:S(2)}) async-start(), calls=%async_computation.3 | async-start | bytes 2506752 | tf_op jit(solution)/shard_map/all_gather | solution.py:110
  164.6 404.0 %reduce-scatter.2.cloned.1.call-start = ((), (), s32[]{:S(2)}) async-start(), calls=%async_computation.4 | async-start | bytes 5013504 | tf_op jit(solution)/shard_map/reduce_scatter | solution.py:142
  167.7 120.1 %copy-start.6 = (pred[256]{0:T(512)(128)(4,1)}, pred[256]{0:T(512)(128)(4,1)S(1)}, u32[]{:S(2)}) copy-start(pred[256]{0:T(512)(128)(4,1)S(1)} %add_compare_fusion) | copy-start | bytes 772
  250.4 2.4 copy-start.1
  254.5 37.6 %copy-start.2 = (bf16[256,6,128]{0,2,1:T(8,128)(2,1)}, bf16[256,6,128]{0,2,1:T(8,128)(2,1)S(1)}, u32[]{:S(2)}) copy-start(bf16[256,6,128]{0,2,1:T(8,128)(2,1)S(1)} %fusion.24) | copy-start | bytes 1179652
  293.6 19.3 %collective-permute-start.1 = (bf16[20,1024]{1,0:T(8,128)(2,1)}, bf16[20,1024]{1,0:T(8,128)(2,1)S(1)}, u32[]{:S(2)}, u32[]{:S(2)}) collective-permute-start(bf16[20,1024]{1,0:T(8,128)(2,1)} %get-tuple-element.7), channel_id=1, source_target_pairs={{1,0},{2,1},{3,2},{4,3},{5,4},{6,5},{7,6},{8,7},{9,8},{10,9},{11,1... | collective-permute-start | bytes 122888 | tf_op jit(solution)/shard_map/ppermute | solution.py:25
  296.1 16.7 %collective-permute-start = (bf16[20,1024]{1,0:T(8,128)(2,1)}, bf16[20,1024]{1,0:T(8,128)(2,1)S(1)}, u32[]{:S(2)}, u32[]{:S(2)}) collective-permute-start(bf16[20,1024]{1,0:T(8,128)(2,1)} %get-tuple-element.6), channel_id=1, source_target_pairs={{0,1},{1,2},{2,3},{3,4},{4,5},{5,6},{6,7},{7,8},{8,9},{9,10},{10,1... | collective-permute-start | bytes 122888 | tf_op jit(solution)/shard_map/ppermute | solution.py:24
  323.5 20.1 %copy-start.5 = (f32[1024]{0:T(1024)S(1)}, f32[1024]{0:T(1024)}, u32[]{:S(2)}) copy-start(f32[1024]{0:T(1024)} %param.17) | copy-start | bytes 12292
  345.3 62.8 %collective-permute-start.3 = (bf16[5,1024]{1,0:T(8,128)(2,1)S(1)}, bf16[5,1024]{1,0:T(8,128)(2,1)S(1)}, u32[]{:S(2)}, u32[]{:S(2)}) collective-permute-start(bf16[5,1024]{1,0:T(8,128)(2,1)S(1)} %get-tuple-element.9), channel_id=1, source_target_pairs={{1,0},{2,1},{3,2},{4,3},{5,4},{6,5},{7,6},{8,7},{9,8},{10,9},{11,1... | collective-permute-start | bytes 30728 | tf_op jit(solution)/shard_map/ppermute | solution.py:25
  351.4 56.8 %collective-permute-start.2 = (bf16[5,1024]{1,0:T(8,128)(2,1)S(1)}, bf16[5,1024]{1,0:T(8,128)(2,1)S(1)}, u32[]{:S(2)}, u32[]{:S(2)}) collective-permute-start(bf16[5,1024]{1,0:T(8,128)(2,1)S(1)} %get-tuple-element.8), channel_id=1, source_target_pairs={{0,1},{1,2},{2,3},{3,4},{4,5},{5,6},{6,7},{7,8},{8,9},{9,10},{10,1... | collective-permute-start | bytes 30728 | tf_op jit(solution)/shard_map/ppermute | solution.py:24
  464.0 7.7 %copy-start.3 = (bf16[256,6,128]{0,2,1:T(8,128)(2,1)S(1)}, bf16[256,6,128]{0,2,1:T(8,128)(2,1)}, u32[]{:S(2)}) copy-start(bf16[256,6,128]{0,2,1:T(8,128)(2,1)} %copy-done.2) | copy-start | bytes 1179652
  464.0 7.7 %copy-start.7 = (pred[256]{0:T(512)(128)(4,1)S(1)}, pred[256]{0:T(512)(128)(4,1)}, u32[]{:S(2)}) copy-start(pred[256]{0:T(512)(128)(4,1)} %copy-done.6) | copy-start | bytes 772
  476.6 228.9 %all-reduce.2.cloned.1.call-start = ((), (), s32[]{:S(2)}) async-start(), calls=%async_computation.5 | async-start | bytes 589824 | tf_op jit(solution)/shard_map/psum | solution.py:141
Sparse Core Ops, SparseCore 0:
  163.9 68.7 all-gather.2
  235.5 52.2 all-gather.4
  476.7 91.8 reduce-scatter.1
  571.2 134.1 all-reduce.1
